TPU v7x, 32 devices: a whole 2x2x4 slice. The times are simulated.
32 devices in a mesh: row: 8 (over y, x, core), col: 4 (over z).
Axes of the slice: x: 2, y: 2, z: 4, core: 2. Of those that a mesh axis runs over, the one named last changes fastest.
Arguments:
- pixels: float32 [8, 3, 1024, 2048], P(None, None, 'row', 'col'), may hold values from -6 to 6
- factor: float32 [1024, 512], P('row'), may hold values from -6 to 6
Outputs:
- gram: float32 [1024, 1024], P('row', 'col')
- projected: float32 [1024, 512], P('col', 'row')
All inputs are finite; a program needn't handle non-finite values.
Results may differ from a plain program's by a relative error of at most 0.000075.
Values sent between devices are 32-bit elements; how exact they have to be, the bound alone decides.
A program may use at most 64 MiB of HBM per device.

v0:
```python
import jax
import jax.numpy as jnp
from jax import lax
from jax.sharding import PartitionSpec as P


def pair_rows(own, others):
    return jnp.einsum(
        "vciw,vcjw->ij",
        own,
        others,
        precision=lax.Precision.HIGHEST,
        preferred_element_type=jnp.float32,
    )


def shards(pixels, factor):
    col_count = lax.axis_size("col")
    row_count = lax.axis_size("row")
    weight_scale = 1.0 / (pixels.shape[0] * pixels.shape[1] * pixels.shape[3] * col_count)
    row_block = pixels.shape[2]
    slices = lax.all_to_all(pixels, "row", split_axis=3, concat_axis=2, tiled=True)
    partial_value = pair_rows(slices, slices) * weight_scale
    total_rows = partial_value.shape[0]
    width = total_rows // col_count
    arranged = partial_value.reshape(row_count, row_block, col_count, width)
    arranged = jnp.transpose(arranged, (0, 2, 1, 3)).reshape(
        row_count * col_count * row_block, width
    )
    block = lax.psum_scatter(arranged, ("row", "col"), scatter_dimension=0, tiled=True)
    term = lax.dot_general(
        block,
        factor,
        (((0,), (0,)), ((), ())),
        precision=lax.Precision.HIGHEST,
        preferred_element_type=jnp.float32,
    )
    summed_term = lax.psum(term, "row")
    share = summed_term.shape[1] // row_count
    projected = lax.dynamic_slice_in_dim(summed_term, lax.axis_index("row") * share, share, 1)
    return (block, projected)


def solution(mesh):
    in_specs = (P(None, None, "row", "col"), P("row", None))
    out_specs = (P("row", "col"), P("col", "row"))
    return jax.shard_map(shards, mesh=mesh, in_specs=in_specs, out_specs=out_specs, check_vma=False)
```

profile of v0, /device:TPU:0, one launch (start us, length us, event | category | flops | bytes accessed | tf_op | source)
XLA Modules:
  0.0 352.7 jit_solution(16188297670045878105)
XLA Ops:
  7.2 0.0 copy-start
  7.2 0.0 reduce-scatter.2.cloned.1.call-start
  7.2 6.6 %copy.13 = f32[8,3,128,512]{2,0,1,3:T(8,128)} copy(f32[8,3,128,512]{3,2,1,0:T(8,128)} %param.2) | data formatting | bytes 12582912 | tf_op args[0]
  13.8 76.7 %all_to_all.18 = f32[8,3,128,512]{2,0,1,3:T(8,128)S(1)} all-to-all(f32[8,3,128,512]{2,0,1,3:T(8,128)} %copy.13), channel_id=1, replica_groups=mesh['row'=8,'col'=4] {'row'}, dimensions={3} | all-to-all | bytes 12582912 | tf_op jit(solution)/shard_map/all_to_all | solution.py:22
  90.5 6.3 %copy.15 = f32[8,3,8,128,64]{3,2,4,0,1:T(8,128)} copy(f32[8,3,8,128,64]{3,0,1,4,2:T(8,128)S(1)} %bitcast.17) | data formatting | bytes 12582912 | tf_op jit(solution)/shard_map/all_to_all | solution.py:22
  96.9 7.1 %all_to_all.16 = f32[8,3,1024,64]{2,3,0,1:T(8,128)} reshape(f32[8,3,8,128,64]{3,2,4,0,1:T(8,128)} %copy.15) | data formatting | bytes 12582912 | tf_op jit(solution)/shard_map/all_to_all | solution.py:22
  103.9 25.1 %bitcast_multiply_fusion = f32[1024,1024]{1,0:T(8,128)} fusion(f32[8,3,1024,64]{2,3,0,1:T(8,128)} %all_to_all.16), kind=kOutput, calls=%fused_computation | convolution fusion | flops 19328401408 | bytes 10485760 | tf_op jit(solution)/shard_map/vciw,vcjw->ij/dot_general | solution.py:8
  129.0 5.6 %reshape.10 = f32[8,128,4,256]{3,2,1,0:T(4,128)} reshape(f32[1024,1024]{1,0:T(8,128)} %bitcast_multiply_fusion) | data formatting | bytes 8388608 | tf_op jit(solution)/shard_map/reshape | solution.py:26
  134.6 4.9 %copy.16 = f32[8,4,128,256]{3,2,1,0:T(8,128)} copy(f32[8,4,128,256]{3,1,2,0:T(4,128)} %bitcast.19) | data formatting | bytes 8388608 | tf_op jit(solution)/shard_map/transpose | solution.py:27
  139.5 0.0 reduce-scatter.2.cloned.1.call-update
  139.5 0.0 all-reduce.2.cloned.1.call-start
  139.6 148.6 %reduce-scatter.2.cloned.1.call-done = f32[128,256]{1,0:T(8,128)} async-done(((f32[4096,256]{1,0:T(8,128)}), f32[128,256]{1,0:T(8,128)}) %reduce-scatter.2.cloned.1.call-update) | async-done | bytes 131088 | tf_op jit(solution)/shard_map/reduce_scatter | solution.py:30
  288.2 0.0 copy-done
  288.2 2.3 fusion
  290.5 0.0 all-reduce.2.cloned.1.call-update
  290.5 53.9 %all-reduce.2.cloned.1.call-done = f32[256,512]{0,1:T(8,128)} async-done(((f32[256,512]{0,1:T(8,128)}), f32[256,512]{0,1:T(8,128)}) %all-reduce.2.cloned.1.call-update) | async-done | bytes 524304 | tf_op jit(solution)/shard_map/psum | solution.py:38
  344.4 1.5 constant_dynamic-slice_fusion
Async XLA Ops:
  7.2 281.0 %copy-start = (f32[128,512]{1,0:T(8,128)S(1)}, f32[128,512]{1,0:T(8,128)}, u32[]{:S(2)}) copy-start(f32[128,512]{1,0:T(8,128)} %param.3) | copy-start | bytes 786436
  7.2 281.0 %reduce-scatter.2.cloned.1.call-start = ((), (), s32[]{:S(2)}) async-start(), calls=%async_computation.2 | async-start | bytes 4325376 | tf_op jit(solution)/shard_map/reduce_scatter | solution.py:30
  139.5 204.9 %all-reduce.2.cloned.1.call-start = ((), (), s32[]{:S(2)}) async-start(), calls=%async_computation.3 | async-start | bytes 1048576 | tf_op jit(solution)/shard_map/psum | solution.py:38
Sparse Core Ops, SparseCore 0:
  139.6 148.4 reduce-scatter.1
  291.3 53.0 all-reduce.1
where the time goes:
time: 353 us
  waiting for transfers between devices  203 us (58%)
  blocking collectives  76.7 us (22%)
  local copies, waits for them, and re-layouts  32 us (9%)
  matrix products  27.4 us (8%)
  between operations  14.1 us (4%)
    reduce_scatter x1, waiting for transfers between devices, shards(): lax.psum_scatter(arranged, ('row', 'col'), scatter_dimension=0, tiled=True)  149 us
    all_to_all x1, blocking collectives, shards(): lax.all_to_all(pixels, 'row', split_axis=3, concat_axis=2, tiled=True)  76.7 us
    psum x1, waiting for transfers between devices, shards(): summed_term = lax.psum(term, 'row')  53.9 us
    dot_general x1, matrix products, pair_rows(): jnp.einsum('vciw,vcjw->ij', own, others, precision=lax.Precision.HIGHEST,...  25.1 us
    all_to_all x2, local copies, waits for them, and re-layouts, shards(): lax.all_to_all(pixels, 'row', split_axis=3, concat_axis=2, tiled=True)  13.4 us
  transfers between devices with their start and end apart: 2, of which 2 were waited for; matrix products, arithmetic and copies ran while one was open for 0% of the time, Pallas kernels for 0%

commit v1 on v0

v1 whole, which is shorter than its diff:
```python
import functools

import jax
import jax.numpy as jnp
from jax import lax
from jax.experimental import pallas as pl
from jax.experimental.pallas import tpu as pltpu
from jax.sharding import PartitionSpec as P

MESH = pl.DeviceIdType.MESH


def flip(value, mask, bits):
    out = 0
    for b in range(bits):
        bit = (value // (1 << b)) % 2
        out = out + (1 << b) * ((1 - bit) if (mask >> b) & 1 else bit)
    return out


def differ(left, right, bits):
    out = 0
    for b in range(bits):
        out = out + (1 << b) * (((left // (1 << b)) + (right // (1 << b))) % 2)
    return out


def dot_t(a, b):
    return lax.dot_general(a, b, (((1,), (1,)), ((), ())), preferred_element_type=jnp.float32)


def kernel(
    rows, cols, scale,
    pix, fac, gram, proj,
    xs, hi, lo, part, pair_in, summed, z_in, plane_out, plane_in, term, term_in,
    own_sem, a_send, a_recv, p_send, p_recv, z_send, z_recv, g_send, g_recv, t_send, t_recv,
):
    r = lax.axis_index("row")
    z = lax.axis_index("col")
    core = r % 2
    chip = r // 2
    rbits = rows.bit_length() - 1
    zbits = cols.bit_length() - 1
    chips = rows // 2
    per = pix.shape[0] // rows
    block = pix.shape[1]
    depth = pix.shape[2]
    mate = [flip(r, k, rbits) for k in range(rows)]

    barrier = pltpu.get_barrier_semaphore()
    for k in range(1, rows):
        pl.semaphore_signal(barrier, inc=1, device_id=(mate[k], z), device_id_type=MESH)
    for k in range(1, cols):
        pl.semaphore_signal(barrier, inc=1, device_id=(r, flip(z, k, zbits)), device_id_type=MESH)
    own = pltpu.make_async_copy(pix.at[pl.ds(r * per, per)], xs.at[0], own_sem)
    own.start()
    pl.semaphore_wait(barrier, rows + cols - 2)

    order = sorted(range(1, rows), key=lambda k: (bin(k >> 1).count("1"), k % 2, k))
    a2a = {}
    for k in order:
        a2a[k] = pltpu.make_async_remote_copy(
            src_ref=pix.at[pl.ds(mate[k] * per, per)],
            dst_ref=xs.at[k],
            send_sem=a_send.at[k],
            recv_sem=a_recv.at[k],
            device_id=(mate[k], z),
            device_id_type=MESH,
        )
        a2a[k].start()

    def split(k):
        for p in range(per):
            x = xs[k, p]
            h = x.astype(jnp.bfloat16)
            at = (k // 2, slice((k % 2) * block, (k % 2 + 1) * block), slice(p * depth, (p + 1) * depth))
            hi[at] = h
            lo[at] = (x - h.astype(jnp.float32)).astype(jnp.bfloat16)

    def pair_copy(i, j):
        return pltpu.make_async_remote_copy(
            src_ref=part.at[i, j, 1],
            dst_ref=pair_in.at[i, j],
            send_sem=p_send.at[i, j],
            recv_sem=p_recv.at[i, j],
            device_id=(mate[1], z),
            device_id_type=MESH,
        )

    def z_copy(i, j):
        zt = flip(chip, j, zbits)
        k = differ(z, zt, zbits)
        return zt, pltpu.make_async_remote_copy(
            src_ref=summed.at[i, j],
            dst_ref=z_in.at[k, i],
            send_sem=z_send.at[i, j],
            recv_sem=z_recv.at[k, i],
            device_id=(r, zt),
            device_id_type=MESH,
        )

    def put(i, j, value):
        part[i, j, 0] = value[:block]
        part[i, j, 1] = value[block:]
        pair_copy(i, j).start()

    for g in range(chips):
        for k in (2 * g, 2 * g + 1):
            if k == 0:
                own.wait()
            else:
                a2a[k].wait_recv()
            split(k)
        fresh = []
        for i in range(g):
            value = dot_t(hi[i], hi[g]) + dot_t(hi[i], lo[g]) + dot_t(lo[i], hi[g])
            put(i, g, value)
            put(g, i, value.T)
            fresh += [(i, g), (g, i)]
        put(g, g, dot_t(hi[g], hi[g]) + dot_t(hi[g], lo[g]) + dot_t(lo[g], hi[g]))
        fresh.append((g, g))
        for i, j in fresh:
            pair_copy(i, j).wait_recv()
            summed[i, j, :, :block] = part[i, j, 0, :, :block] + pair_in[i, j, :, block:]
            summed[i, j, :, block:] = part[i, j, 0, :, block:] + pair_in[i, j, :, :block]
            zt, copy = z_copy(i, j)

            @pl.when(zt != z)
            def _():
                copy.start()

    mine = differ(chip, z, zbits)

    def plane_copy(i):
        return pltpu.make_async_remote_copy(
            src_ref=plane_out.at[i],
            dst_ref=plane_in.at[i],
            send_sem=g_send.at[i],
            recv_sem=g_recv.at[i],
            device_id=(mate[2 * i], z),
            device_id_type=MESH,
        )

    for i in list(range(1, chips)) + [0]:
        total = summed[i, mine]
        for k in range(1, cols):
            pltpu.make_async_remote_copy(
                src_ref=summed.at[i, 0],
                dst_ref=z_in.at[k, i],
                send_sem=z_send.at[i, 0],
                recv_sem=z_recv.at[k, i],
                device_id=(r, flip(z, k, zbits)),
                device_id_type=MESH,
            ).wait_recv()
            total = total + z_in[k, i]
        plane_out[i] = total
        if i > 0:
            plane_copy(i).start()
    total = plane_out[0]
    for i in range(1, chips):
        plane_copy(i).wait_recv()
        total = total + plane_in[i]
    total = total * scale
    first = pl.multiple_of(core * block, block)
    second = pl.multiple_of((1 - core) * block, block)
    gram[:, pl.ds(first, block)] = total[:, :block]
    gram[:, pl.ds(second, block)] = total[:, block:]

    value = lax.dot_general(
        fac[...], gram[...], (((0,), (0,)), ((), ())),
        precision=lax.Precision.HIGHEST, preferred_element_type=jnp.float32,
    )
    share = value.shape[0] // rows
    for k in range(rows):
        term[k] = value[k * share:(k + 1) * share]

    def term_copy(k):
        return pltpu.make_async_remote_copy(
            src_ref=term.at[mate[k]],
            dst_ref=term_in.at[k],
            send_sem=t_send.at[k],
            recv_sem=t_recv.at[k],
            device_id=(mate[k], z),
            device_id_type=MESH,
        )

    for k in range(rows - 1, 0, -1):
        term_copy(k).start()
    total = term[r]
    for k in range(1, rows):
        term_copy(k).wait_recv()
        total = total + term_in[k]
    proj[...] = total.T

    for k in range(1, rows):
        a2a[k].wait_send()
        term_copy(k).wait_send()
    for i in range(chips):
        for j in range(chips):
            pair_copy(i, j).wait_send()
            zt, copy = z_copy(i, j)

            @pl.when(zt != z)
            def _():
                copy.wait_send()
        if i > 0:
            plane_copy(i).wait_send()


def fused(pixels, factor):
    rows, cols = lax.axis_size("row"), lax.axis_size("col")
    views, colours, block, depth = pixels.shape
    count = views * colours
    per = count // rows
    chips = rows // 2
    rank = factor.shape[1]
    scale = 1.0 / (count * depth * cols)
    vmem, dma = pltpu.VMEM, pltpu.SemaphoreType.DMA
    f32 = jnp.float32
    return pl.pallas_call(
        functools.partial(kernel, rows, cols, scale),
        out_shape=(
            jax.ShapeDtypeStruct((block, 2 * block), f32),
            jax.ShapeDtypeStruct((2 * block, rank // rows), f32),
        ),
        in_specs=[pl.BlockSpec(memory_space=pl.ANY), pl.BlockSpec(memory_space=pltpu.VMEM)],
        out_specs=(pl.BlockSpec(memory_space=pltpu.VMEM), pl.BlockSpec(memory_space=pltpu.VMEM)),
        scratch_shapes=[
            vmem((rows, per, block, depth), f32),
            vmem((chips, 2 * block, per * depth), jnp.bfloat16),
            vmem((chips, 2 * block, per * depth), jnp.bfloat16),
            vmem((chips, chips, 2, block, 2 * block), f32),
            vmem((chips, chips, block, 2 * block), f32),
            vmem((chips, chips, block, 2 * block), f32),
            vmem((cols, chips, block, 2 * block), f32),
            vmem((chips, block, 2 * block), f32),
            vmem((chips, block, 2 * block), f32),
            vmem((rows, rank // rows, 2 * block), f32),
            vmem((rows, rank // rows, 2 * block), f32),
            dma,
            dma((rows,)), dma((rows,)),
            dma((chips, chips)), dma((chips, chips)),
            dma((chips, chips)), dma((cols, chips)),
            dma((chips,)), dma((chips,)),
            dma((rows,)), dma((rows,)),
        ],
        compiler_params=pltpu.CompilerParams(
            collective_id=0, has_side_effects=True, vmem_limit_bytes=56 * 1024 * 1024
        ),
    )(pixels.reshape(count, block, depth), factor)


def pair_rows(own, others):
    return jnp.einsum(
        "vciw,vcjw->ij", own, others, precision=lax.Precision.HIGHEST, preferred_element_type=jnp.float32
    )


def general(pixels, factor):
    col_count = lax.axis_size("col")
    row_count = lax.axis_size("row")
    weight_scale = 1.0 / (pixels.shape[0] * pixels.shape[1] * pixels.shape[3] * col_count)
    row_block = pixels.shape[2]
    slices = lax.all_to_all(pixels, "row", split_axis=3, concat_axis=2, tiled=True)
    partial_value = pair_rows(slices, slices) * weight_scale
    width = partial_value.shape[0] // col_count
    arranged = partial_value.reshape(row_count, row_block, col_count, width)
    arranged = jnp.transpose(arranged, (0, 2, 1, 3)).reshape(row_count * col_count * row_block, width)
    block = lax.psum_scatter(arranged, ("row", "col"), scatter_dimension=0, tiled=True)
    term = lax.dot_general(
        block, factor, (((0,), (0,)), ((), ())),
        precision=lax.Precision.HIGHEST, preferred_element_type=jnp.float32,
    )
    summed_term = lax.psum(term, "row")
    share = summed_term.shape[1] // row_count
    projected = lax.dynamic_slice_in_dim(summed_term, lax.axis_index("row") * share, share, 1)
    return (block, projected)


def shards(pixels, factor):
    rows, cols = lax.axis_size("row"), lax.axis_size("col")
    views, colours, block, depth = pixels.shape
    fits = (
        rows == 2 * cols
        and rows & (rows - 1) == 0
        and (views * colours) % rows == 0
        and block % 128 == 0
        and depth % 128 == 0
        and factor.shape[1] % (8 * rows) == 0
        and 8 * rows * block * (views * colours // rows) * depth <= 16 * 1024 * 1024
    )
    return (fused if fits else general)(pixels, factor)


def solution(mesh):
    in_specs = (P(None, None, "row", "col"), P("row", None))
    out_specs = (P("row", "col"), P("col", "row"))
    return jax.shard_map(shards, mesh=mesh, in_specs=in_specs, out_specs=out_specs, check_vma=False)
```

time: 353 us -> 135 us (0.38)
  waiting for transfers between devices: 203 us -> 0 us
  Pallas kernels: 0 us -> 131 us
  blocking collectives: 76.7 us -> 0 us
  local copies, waits for them, and re-layouts: 32 us -> 3.18 us
  matrix products: 27.4 us -> 0 us
  between operations: 14.1 us -> 0.64 us
    reduce_scatter x1 -> x0, waiting for transfers between devices: 149 us -> none  [shards(): lax.psum_scatter(arranged, ('row', 'col'), scatter_dimension=0, tiled=True)]
    pallas_call x0 -> x1, Pallas kernels: none -> 131 us  [fused(): pl.pallas_call(functools.partial(kernel, rows, cols, scale), out_shape=(j...]
    all_to_all x1 -> x0, blocking collectives: 76.7 us -> none  [shards(): lax.all_to_all(pixels, 'row', split_axis=3, concat_axis=2, tiled=True)]
    psum x1 -> x0, waiting for transfers between devices: 53.9 us -> none  [shards(): summed_term = lax.psum(term, 'row')]
    dot_general x2 -> x0, matrix products: 27.4 us -> none  [the longest x1 25.1 us: pair_rows(): jnp.einsum('vciw,vcjw->ij', own, others, precision=lax.Precision.HIGHEST,...]
    all_to_all x2 -> x0, local copies, waits for them, and re-layouts: 13.4 us -> none  [shards(): lax.all_to_all(pixels, 'row', split_axis=3, concat_axis=2, tiled=True)]
    reshape x1 -> x0, local copies, waits for them, and re-layouts: 5.62 us -> none  [shards(): arranged = partial_value.reshape(row_count, row_block, col_count, width)]
    unnamed x3 -> x1, local copies, waits for them, and re-layouts: 6.63 us -> 1.57 us
  transfers between devices with their start and end apart: 2 -> 0, of which waited for: 2 -> 0; matrix products, arithmetic and copies ran while one was open for 0% -> 0% of each run, Pallas kernels for 0% -> 0%
where the time goes in v1:
time: 135 us
  Pallas kernels  131 us (97%)
  local copies, waits for them, and re-layouts  3.18 us (2%)
    pallas_call x1, Pallas kernels, fused(): pl.pallas_call(functools.partial(kernel, rows, cols, scale), out_shape=(j...  131 us

profile of v1, /device:TPU:0, one launch (start us, length us, event | category | flops | bytes accessed | tf_op | source)
XLA Modules:
  0.0 134.6 jit_solution(11156271935405046688)
XLA Ops:
  0.6 130.8 %shard_map.41 = (f32[128,256]{1,0:T(8,128)}, f32[256,64]{1,0:T(8,128)}) custom-call(f32[24,128,512]{2,1,0:T(8,128)} %bitcast.1, f32[128,512]{1,0:T(8,128)} %fac.1), custom_call_target="tpu_custom_call" | custom-call | tf_op jit(solution)/shard_map/pallas_call | solution.py:220
  131.4 1.6 %copy.4 = f32[256,64]{0,1:T(8,128)} copy(f32[256,64]{1,0:T(8,128)} %get-tuple-element.3) | data formatting | bytes 131072 | tf_op jit(solution)/shard_map/pallas_call | solution.py:220
  133.0 1.6 %copy.6 = f32[128,256]{1,0:T(8,128)} copy(f32[128,256]{1,0:T(8,128)} %get-tuple-element.6) | data formatting | bytes 262144

commit v2 on v1

--- a/solution.py
+++ b/solution.py
@@ -32,8 +32,9 @@
 def kernel(
     rows, cols, scale,
     pix, fac, gram, proj,
-    xs, hi, lo, part, pair_in, summed, z_in, plane_out, plane_in, term, term_in,
-    own_sem, a_send, a_recv, p_send, p_recv, z_send, z_recv, g_send, g_recv, t_send, t_recv,
+    xs, hi, lo, part, pair_in, summed, z_in, plane_out, plane_in, late_in, late_sum, zl_in, term, term_in,
+    own_sem, a_send, a_recv, p_send, p_recv, z_send, z_recv, g_send, g_recv,
+    l_send, l_recv, zl_send, zl_recv, t_send, t_recv,
 ):
     r = lax.axis_index("row")
     z = lax.axis_index("col")
@@ -42,6 +43,8 @@
     rbits = rows.bit_length() - 1
     zbits = cols.bit_length() - 1
     chips = rows // 2
+    last = chips - 1
+    mine = differ(chip, z, zbits)
     per = pix.shape[0] // rows
     block = pix.shape[1]
     depth = pix.shape[2]
@@ -67,7 +70,8 @@
             device_id=(mate[k], z),
             device_id_type=MESH,
         )
-        a2a[k].start()
+        if k < 2 * last:
+            a2a[k].start()
 
     def split(k):
         for p in range(per):
@@ -103,6 +107,38 @@
         part[i, j, 0] = value[:block]
         part[i, j, 1] = value[block:]
         pair_copy(i, j).start()
+
+    def late_copy(i, j):
+        return pltpu.make_async_remote_copy(
+            src_ref=summed.at[i, j],
+            dst_ref=late_in.at[i, i ^ j],
+            send_sem=l_send.at[i, i ^ j],
+            recv_sem=l_recv.at[i, i ^ j],
+            device_id=(mate[2 * i], z),
+            device_id_type=MESH,
+        )
+
+    def z_late_copy(m):
+        zt = flip(chip, m, zbits)
+        k = differ(z, zt, zbits)
+        return zt, pltpu.make_async_remote_copy(
+            src_ref=late_sum.at[m],
+            dst_ref=zl_in.at[k],
+            send_sem=zl_send.at[m],
+            recv_sem=zl_recv.at[k],
+            device_id=(r, zt),
+            device_id_type=MESH,
+        )
+
+    def plane_copy(i):
+        return pltpu.make_async_remote_copy(
+            src_ref=plane_out.at[i],
+            dst_ref=plane_in.at[i],
+            send_sem=g_send.at[i],
+            recv_sem=g_recv.at[i],
+            device_id=(mate[2 * i], z),
+            device_id_type=MESH,
+        )
 
     for g in range(chips):
         for k in (2 * g, 2 * g + 1):
@@ -114,52 +150,86 @@
         fresh = []
         for i in range(g):
             value = dot_t(hi[i], hi[g]) + dot_t(hi[i], lo[g]) + dot_t(lo[i], hi[g])
+            put(g, i, value.T)
             put(i, g, value)
-            put(g, i, value.T)
-            fresh += [(i, g), (g, i)]
+            fresh += [(g, i), (i, g)]
         put(g, g, dot_t(hi[g], hi[g]) + dot_t(hi[g], lo[g]) + dot_t(lo[g], hi[g]))
         fresh.append((g, g))
+        if g == 0:
+            for k in order:
+                if 2 <= k < 2 * last:
+                    a2a[k].wait_send()
+            for k in (2 * last, 2 * last + 1):
+                a2a[k].start()
         for i, j in fresh:
             pair_copy(i, j).wait_recv()
             summed[i, j, :, :block] = part[i, j, 0, :, :block] + pair_in[i, j, :, block:]
             summed[i, j, :, block:] = part[i, j, 0, :, block:] + pair_in[i, j, :, :block]
-            zt, copy = z_copy(i, j)
-
-            @pl.when(zt != z)
-            def _():
-                copy.start()
-
-    mine = differ(chip, z, zbits)
-
-    def plane_copy(i):
-        return pltpu.make_async_remote_copy(
-            src_ref=plane_out.at[i],
-            dst_ref=plane_in.at[i],
-            send_sem=g_send.at[i],
-            recv_sem=g_recv.at[i],
-            device_id=(mate[2 * i], z),
-            device_id_type=MESH,
-        )
-
-    for i in list(range(1, chips)) + [0]:
-        total = summed[i, mine]
-        for k in range(1, cols):
-            pltpu.make_async_remote_copy(
-                src_ref=summed.at[i, 0],
-                dst_ref=z_in.at[k, i],
-                send_sem=z_send.at[i, 0],
-                recv_sem=z_recv.at[k, i],
-                device_id=(r, flip(z, k, zbits)),
-                device_id_type=MESH,
-            ).wait_recv()
-            total = total + z_in[k, i]
-        plane_out[i] = total
+            if g == last:
+                if i > 0:
+                    late_copy(i, j).start()
+            else:
+                zt, copy = z_copy(i, j)
+
+                @pl.when(zt != z)
+                def _():
+                    copy.start()
+
+    for i in list(range(1, last)) + [0]:
+        @pl.when(mine < last)
+        def _():
+            total = summed[i, mine]
+            for k in range(1, cols):
+                pltpu.make_async_remote_copy(
+                    src_ref=summed.at[i, 0],
+                    dst_ref=z_in.at[k, i],
+                    send_sem=z_send.at[i, 0],
+                    recv_sem=z_recv.at[k, i],
+                    device_id=(r, flip(z, k, zbits)),
+                    device_id_type=MESH,
+                ).wait_recv()
+                total = total + z_in[k, i]
+            plane_out[i] = total
+
+        @pl.when(mine == last)
+        def _():
+            plane_out[i] = jnp.zeros((block, 2 * block), jnp.float32)
+
         if i > 0:
             plane_copy(i).start()
+
+    for m in range(last, -1, -1):
+        sources = {last, last ^ m}
+        total = None
+        for i in sorted(sources):
+            if i == 0:
+                piece = summed[0, last]
+            else:
+                late_copy(i, i ^ m).wait_recv()
+                piece = late_in[i, m]
+            total = piece if total is None else total + piece
+        late_sum[m] = total
+        zt, copy = z_late_copy(m)
+
+        @pl.when(zt != z)
+        def _():
+            copy.start()
+
     total = plane_out[0]
-    for i in range(1, chips):
+    for i in range(1, last):
         plane_copy(i).wait_recv()
         total = total + plane_in[i]
+    total = total + late_sum[mine]
+    for k in range(1, cols):
+        pltpu.make_async_remote_copy(
+            src_ref=late_sum.at[0],
+            dst_ref=zl_in.at[k],
+            send_sem=zl_send.at[0],
+            recv_sem=zl_recv.at[k],
+            device_id=(r, flip(z, k, zbits)),
+            device_id_type=MESH,
+        ).wait_recv()
+        total = total + zl_in[k]
     total = total * scale
     first = pl.multiple_of(core * block, block)
     second = pl.multiple_of((1 - core) * block, block)
@@ -193,18 +263,27 @@
     proj[...] = total.T
 
     for k in range(1, rows):
-        a2a[k].wait_send()
+        if k < 2 or k >= 2 * last:
+            a2a[k].wait_send()
         term_copy(k).wait_send()
     for i in range(chips):
         for j in range(chips):
             pair_copy(i, j).wait_send()
-            zt, copy = z_copy(i, j)
-
-            @pl.when(zt != z)
-            def _():
-                copy.wait_send()
-        if i > 0:
+            if i < last and j < last:
+                zt, copy = z_copy(i, j)
+
+                @pl.when(zt != z)
+                def _():
+                    copy.wait_send()
+            elif i > 0:
+                late_copy(i, j).wait_send()
+        if 0 < i < last:
             plane_copy(i).wait_send()
+        zt, copy = z_late_copy(i)
+
+        @pl.when(zt != z)
+        def _():
+            copy.wait_send()
 
 
 def fused(pixels, factor):
@@ -235,6 +314,9 @@
             vmem((cols, chips, block, 2 * block), f32),
             vmem((chips, block, 2 * block), f32),
             vmem((chips, block, 2 * block), f32),
+            vmem((chips, chips, block, 2 * block), f32),
+            vmem((chips, block, 2 * block), f32),
+            vmem((cols, block, 2 * block), f32),
             vmem((rows, rank // rows, 2 * block), f32),
             vmem((rows, rank // rows, 2 * block), f32),
             dma,
@@ -242,6 +324,8 @@
             dma((chips, chips)), dma((chips, chips)),
             dma((chips, chips)), dma((cols, chips)),
             dma((chips,)), dma((chips,)),
+            dma((chips, chips)), dma((chips, chips)),
+            dma((chips,)), dma((cols,)),
             dma((rows,)), dma((rows,)),
         ],
         compiler_params=pltpu.CompilerParams(
@@ -282,6 +366,7 @@
     views, colours, block, depth = pixels.shape
     fits = (
         rows == 2 * cols
+        and rows >= 4
         and rows & (rows - 1) == 0
         and (views * colours) % rows == 0
         and block % 128 == 0

time: 135 us -> 122 us (0.904)
  Pallas kernels: 131 us -> 118 us
    pallas_call x1, Pallas kernels: 131 us -> 118 us  [fused(): pl.pallas_call(functools.partial(kernel, rows, cols, scale), out_shape=(j...]
where the time goes in v2:
time: 122 us
  Pallas kernels  118 us (97%)
  local copies, waits for them, and re-layouts  3.18 us (3%)
    pallas_call x1, Pallas kernels, fused(): pl.pallas_call(functools.partial(kernel, rows, cols, scale), out_shape=(j...  118 us

profile of v2, /device:TPU:0, one launch (start us, length us, event | category | flops | bytes accessed | tf_op | source)
XLA Modules:
  0.0 121.9 jit_solution(9260726455765072179)
XLA Ops:
  0.6 118.1 %shard_map.41 = (f32[128,256]{1,0:T(8,128)}, f32[256,64]{1,0:T(8,128)}) custom-call(f32[24,128,512]{2,1,0:T(8,128)} %bitcast.1, f32[128,512]{1,0:T(8,128)} %fac.1), custom_call_target="tpu_custom_call" | custom-call | tf_op jit(solution)/shard_map/pallas_call | solution.py:299
  118.7 1.6 %copy.4 = f32[256,64]{0,1:T(8,128)} copy(f32[256,64]{1,0:T(8,128)} %get-tuple-element.3) | data formatting | bytes 131072 | tf_op jit(solution)/shard_map/pallas_call | solution.py:299
  120.3 1.6 %copy.6 = f32[128,256]{1,0:T(8,128)} copy(f32[128,256]{1,0:T(8,128)} %get-tuple-element.6) | data formatting | bytes 262144

commit v3 on v2

--- a/solution.py
+++ b/solution.py
@@ -32,8 +32,8 @@
 def kernel(
     rows, cols, scale,
     pix, fac, gram, proj,
-    xs, hi, lo, part, pair_in, summed, z_in, plane_out, plane_in, late_in, late_sum, zl_in, term, term_in,
-    own_sem, a_send, a_recv, p_send, p_recv, z_send, z_recv, g_send, g_recv,
+    xs, hi, lo, part, pair_in, summed, z_in, plane_out, plane_in, late_in, late_sum, zl_in, acc, term, term_in,
+    own_sem, a_send, a_recv, d_send, d_recv, p_send, p_recv, z_send, z_recv, g_send, g_recv,
     l_send, l_recv, zl_send, zl_recv, t_send, t_recv,
 ):
     r = lax.axis_index("row")
@@ -62,19 +62,26 @@
     order = sorted(range(1, rows), key=lambda k: (bin(k >> 1).count("1"), k % 2, k))
     a2a = {}
     for k in order:
-        a2a[k] = pltpu.make_async_remote_copy(
-            src_ref=pix.at[pl.ds(mate[k] * per, per)],
-            dst_ref=xs.at[k],
-            send_sem=a_send.at[k],
-            recv_sem=a_recv.at[k],
-            device_id=(mate[k], z),
-            device_id_type=MESH,
-        )
+        a2a[k] = [
+            pltpu.make_async_remote_copy(
+                src_ref=pix.at[pl.ds(mate[k] * per + p, size)],
+                dst_ref=xs.at[k, pl.ds(p, size)],
+                send_sem=sems[0],
+                recv_sem=sems[1],
+                device_id=(mate[k], z),
+                device_id_type=MESH,
+            )
+            for p, size, sems in (
+                [(0, per, (a_send.at[k], a_recv.at[k]))]
+                if k < 2 * last
+                else [(p, 1, (d_send.at[k % 2, p], d_recv.at[k % 2, p])) for p in range(per)]
+            )
+        ]
         if k < 2 * last:
-            a2a[k].start()
-
-    def split(k):
-        for p in range(per):
+            a2a[k][0].start()
+
+    def split(k, pieces):
+        for p in pieces:
             x = xs[k, p]
             h = x.astype(jnp.bfloat16)
             at = (k // 2, slice((k % 2) * block, (k % 2 + 1) * block), slice(p * depth, (p + 1) * depth))
@@ -140,40 +147,75 @@
             device_id_type=MESH,
         )
 
-    for g in range(chips):
+    def finish(i, j):
+        pair_copy(i, j).wait_recv()
+        summed[i, j, :, :block] = part[i, j, 0, :, :block] + pair_in[i, j, :, block:]
+        summed[i, j, :, block:] = part[i, j, 0, :, block:] + pair_in[i, j, :, :block]
+        if i == last or j == last:
+            if i > 0:
+                late_copy(i, j).start()
+        else:
+            zt, copy = z_copy(i, j)
+
+            @pl.when(zt != z)
+            def _():
+                copy.start()
+
+    def product(i, g, at):
+        return (
+            dot_t(hi[i, :, at], hi[g, :, at])
+            + dot_t(hi[i, :, at], lo[g, :, at])
+            + dot_t(lo[i, :, at], hi[g, :, at])
+        )
+
+    for g in range(last):
         for k in (2 * g, 2 * g + 1):
             if k == 0:
                 own.wait()
             else:
-                a2a[k].wait_recv()
-            split(k)
+                a2a[k][0].wait_recv()
+            split(k, range(per))
         fresh = []
-        for i in range(g):
-            value = dot_t(hi[i], hi[g]) + dot_t(hi[i], lo[g]) + dot_t(lo[i], hi[g])
-            put(g, i, value.T)
+        for i in range(g + 1):
+            value = product(i, g, slice(None))
             put(i, g, value)
-            fresh += [(g, i), (i, g)]
-        put(g, g, dot_t(hi[g], hi[g]) + dot_t(hi[g], lo[g]) + dot_t(lo[g], hi[g]))
-        fresh.append((g, g))
+            fresh.append((i, g))
+            if i < g:
+                put(g, i, value.T)
+                fresh.append((g, i))
         if g == 0:
             for k in order:
                 if 2 <= k < 2 * last:
-                    a2a[k].wait_send()
-            for k in (2 * last, 2 * last + 1):
-                a2a[k].start()
+                    a2a[k][0].wait_send()
+            for p in range(per):
+                for k in (2 * last, 2 * last + 1):
+                    a2a[k][p].start()
         for i, j in fresh:
-            pair_copy(i, j).wait_recv()
-            summed[i, j, :, :block] = part[i, j, 0, :, :block] + pair_in[i, j, :, block:]
-            summed[i, j, :, block:] = part[i, j, 0, :, block:] + pair_in[i, j, :, :block]
-            if g == last:
-                if i > 0:
-                    late_copy(i, j).start()
-            else:
-                zt, copy = z_copy(i, j)
-
-                @pl.when(zt != z)
-                def _():
-                    copy.start()
+            finish(i, j)
+
+    for p in range(per):
+        for k in (2 * last, 2 * last + 1):
+            a2a[k][p].wait_recv()
+            split(k, (p,))
+        at = slice(p * depth, (p + 1) * depth)
+        waiting = []
+        for i in range(chips):
+            value = product(i, last, at)
+            if p > 0:
+                value = value + acc[i]
+            if p < per - 1:
+                acc[i] = value
+                continue
+            fresh = [(i, last)]
+            if i < last:
+                put(last, i, value.T)
+                fresh.insert(0, (last, i))
+            put(i, last, value)
+            for pair in waiting:
+                finish(*pair)
+            waiting = fresh
+        for pair in waiting:
+            finish(*pair)
 
     for i in list(range(1, last)) + [0]:
         @pl.when(mine < last)
@@ -264,7 +306,8 @@
 
     for k in range(1, rows):
         if k < 2 or k >= 2 * last:
-            a2a[k].wait_send()
+            for copy in a2a[k]:
+                copy.wait_send()
         term_copy(k).wait_send()
     for i in range(chips):
         for j in range(chips):
@@ -317,10 +360,12 @@
             vmem((chips, chips, block, 2 * block), f32),
             vmem((chips, block, 2 * block), f32),
             vmem((cols, block, 2 * block), f32),
+            vmem((chips, 2 * block, 2 * block), f32),
             vmem((rows, rank // rows, 2 * block), f32),
             vmem((rows, rank // rows, 2 * block), f32),
             dma,
             dma((rows,)), dma((rows,)),
+            dma((2, per)), dma((2, per)),
             dma((chips, chips)), dma((chips, chips)),
             dma((chips, chips)), dma((cols, chips)),
             dma((chips,)), dma((chips,)),

time: 122 us -> 116 us (0.951)
  Pallas kernels: 118 us -> 112 us
    pallas_call x1, Pallas kernels: 118 us -> 112 us  [fused(): pl.pallas_call(functools.partial(kernel, rows, cols, scale), out_shape=(j...]
where the time goes in v3:
time: 116 us
  Pallas kernels  112 us (97%)
  local copies, waits for them, and re-layouts  3.18 us (3%)
    pallas_call x1, Pallas kernels, fused(): pl.pallas_call(functools.partial(kernel, rows, cols, scale), out_shape=(j...  112 us

profile of v3, /device:TPU:0, one launch (start us, length us, event | category | flops | bytes accessed | tf_op | source)
XLA Modules:
  0.0 115.7 jit_solution(7966307576676951792)
XLA Ops:
  0.6 111.9 %shard_map.41 = (f32[128,256]{1,0:T(8,128)}, f32[256,64]{1,0:T(8,128)}) custom-call(f32[24,128,512]{2,1,0:T(8,128)} %bitcast.1, f32[128,512]{1,0:T(8,128)} %fac.1), custom_call_target="tpu_custom_call" | custom-call | tf_op jit(solution)/shard_map/pallas_call | solution.py:342
  112.5 1.6 %copy.4 = f32[256,64]{0,1:T(8,128)} copy(f32[256,64]{1,0:T(8,128)} %get-tuple-element.3) | data formatting | bytes 131072 | tf_op jit(solution)/shard_map/pallas_call | solution.py:342
  114.1 1.6 %copy.6 = f32[128,256]{1,0:T(8,128)} copy(f32[128,256]{1,0:T(8,128)} %get-tuple-element.6) | data formatting | bytes 262144

commit v4 on v3

--- a/solution.py
+++ b/solution.py
@@ -217,6 +217,23 @@
         for pair in waiting:
             finish(*pair)
 
+    for m in range(last, -1, -1):
+        sources = {last, last ^ m}
+        total = None
+        for i in sorted(sources):
+            if i == 0:
+                piece = summed[0, last]
+            else:
+                late_copy(i, i ^ m).wait_recv()
+                piece = late_in[i, m]
+            total = piece if total is None else total + piece
+        late_sum[m] = total
+        zt, copy = z_late_copy(m)
+
+        @pl.when(zt != z)
+        def _():
+            copy.start()
+
     for i in list(range(1, last)) + [0]:
         @pl.when(mine < last)
         def _():
@@ -239,23 +256,6 @@
 
         if i > 0:
             plane_copy(i).start()
-
-    for m in range(last, -1, -1):
-        sources = {last, last ^ m}
-        total = None
-        for i in sorted(sources):
-            if i == 0:
-                piece = summed[0, last]
-            else:
-                late_copy(i, i ^ m).wait_recv()
-                piece = late_in[i, m]
-            total = piece if total is None else total + piece
-        late_sum[m] = total
-        zt, copy = z_late_copy(m)
-
-        @pl.when(zt != z)
-        def _():
-            copy.start()
 
     total = plane_out[0]
     for i in range(1, last):

time: 116 us -> 116 us (level)
  no operation moved by 1% of the time
where the time goes in v4:
time: 116 us
  Pallas kernels  112 us (97%)
  local copies, waits for them, and re-layouts  3.18 us (3%)
    pallas_call x1, Pallas kernels, fused(): pl.pallas_call(functools.partial(kernel, rows, cols, scale), out_shape=(j...  112 us

profile of v4, /device:TPU:0, one launch (start us, length us, event | category | flops | bytes accessed | tf_op | source)
XLA Modules:
  0.0 115.6 jit_solution(8449503658034968103)
XLA Ops:
  0.6 111.8 %shard_map.41 = (f32[128,256]{1,0:T(8,128)}, f32[256,64]{1,0:T(8,128)}) custom-call(f32[24,128,512]{2,1,0:T(8,128)} %bitcast.1, f32[128,512]{1,0:T(8,128)} %fac.1), custom_call_target="tpu_custom_call" | custom-call | tf_op jit(solution)/shard_map/pallas_call | solution.py:342
  112.4 1.6 %copy.4 = f32[256,64]{0,1:T(8,128)} copy(f32[256,64]{1,0:T(8,128)} %get-tuple-element.3) | data formatting | bytes 131072 | tf_op jit(solution)/shard_map/pallas_call | solution.py:342
  114.0 1.6 %copy.6 = f32[128,256]{1,0:T(8,128)} copy(f32[128,256]{1,0:T(8,128)} %get-tuple-element.6) | data formatting | bytes 262144
